TPU v7x, 512 devices: a whole 4x8x8 slice. The times are simulated.
512 devices in a mesh: pair: 64 (over y, z), intg: 8 (over x, core).
Axes of the slice: x: 4, y: 8, z: 8, core: 2. Of those that a mesh axis runs over, the one named last changes fastest.
Arguments:
- amplitudes: bfloat16 [512, 128, 1024], P('pair'), may hold values from -6 to 6
- integrals: bfloat16 [2048, 128, 1024], P('intg', 'pair'), may hold values from -0.015625 to 0.015625
- tile_irreps: int32 [24], replicated, may hold values from 0 to 1
- screening: int32 [128], replicated, may hold values 0 or 1
- slot_tiles: int32 [128], replicated, may hold values from 0 to 127, each once
- pair_list: int32 [512, 2], P('pair'), may hold values from 0 to 299
- occupied_energy: float32 [300], replicated, may hold values from -1.2 to -0.3
- virtual_energy: float32 [768], replicated, may hold values from 0.2 to 1.5
Outputs:
- update: float32 [512, 2048], P('pair', 'intg')
Inputs may be any that keep to these rules, and one draw needn't show every extreme that they name: slot_tiles names every cd tile pair of the slab exactly once.
All inputs are finite; a program needn't handle non-finite values.
Results may differ from a plain program's by a relative error of at most 0.0003.
Values may be sent and summed in bfloat16 or wider, within the bound.
No kernel may reach another device: no remote copies, remote signals or barrier semaphores. Data moves between devices by JAX's collectives and lax.ppermute only.
A program may use at most 64 MiB of HBM per device.

v0:
```python
import jax
import jax.numpy as jnp
from jax import lax
from jax.sharding import PartitionSpec as P

TILE = 32
NT = 24


def lookup(table, index):
    places = jnp.arange(table.shape[0], dtype=jnp.int32)
    return jnp.sum(jnp.where(places[None, :] == index[:, None], table[None, :], 0), axis=1)


def on_device(
    amplitudes,
    integrals,
    tile_irreps,
    screening,
    slot_tiles,
    pair_list,
    occupied_energy,
    virtual_energy,
):
    slots_here = integrals.shape[1]
    ab_rows = integrals.shape[0]
    block = lax.axis_index("intg")
    owner = lax.axis_index("pair")
    first_tile = block // NT
    second_tile = block % NT
    sym_ab = jnp.bitwise_xor(
        lookup(tile_irreps, first_tile[None]), lookup(tile_irreps, second_tile[None])
    )
    my_slots = lax.dynamic_slice_in_dim(slot_tiles, owner * slots_here, slots_here)
    sym_cd = jnp.bitwise_xor(
        lookup(tile_irreps, my_slots // NT), lookup(tile_irreps, my_slots % NT)
    )
    keep = jnp.where(sym_cd == sym_ab, 1.0, 0.0).astype(jnp.float32) * lookup(
        screening, my_slots
    ).astype(jnp.float32)
    ordered = jnp.take(amplitudes, slot_tiles, axis=1)
    columns = lax.all_to_all(ordered, "pair", split_axis=1, concat_axis=0, tiled=True)
    masked_ints = integrals * keep.astype(jnp.bfloat16)[None, :, None]
    ladder = lax.psum_scatter(
        lax.dot_general(
            columns, masked_ints, (((1, 2), (1, 2)), ((), ())), preferred_element_type=jnp.float32
        ),
        "pair",
        scatter_dimension=0,
        tiled=True,
    )
    occupied_sum = lookup(occupied_energy, pair_list[:, 0]) + lookup(
        occupied_energy, pair_list[:, 1]
    )
    first_energy = lax.dynamic_slice_in_dim(virtual_energy, first_tile * TILE, TILE)
    second_energy = lax.dynamic_slice_in_dim(virtual_energy, second_tile * TILE, TILE)
    virtual_sum = jnp.repeat(first_energy[: ab_rows // TILE], TILE) + jnp.tile(
        second_energy, ab_rows // TILE
    )
    denom = occupied_sum[:, None] - virtual_sum[None, :]
    return ladder / denom


def solution(mesh):
    placed = (
        P("pair", None, None),
        P("intg", "pair", None),
        P(),
        P(),
        P(),
        P("pair", None),
        P(),
        P(),
    )
    return jax.shard_map(
        on_device, mesh=mesh, in_specs=placed, out_specs=P("pair", "intg"), check_vma=False
    )
```

profile of v0, /device:TPU:2, one launch (start us, length us, event | category | flops | bytes accessed | tf_op | source)
XLA Modules:
  0.0 256.4 jit_solution(17313821855280942886)
XLA Ops:
  6.5 0.0 copy-start
  6.5 0.8 compare_select_fusion
  7.3 0.7 compare_and_fusion
  8.0 0.1 copy-done
  8.1 8.1 %gather_fusion = bf16[128,8,1024]{2,0,1:T(8,128)(2,1)} fusion(bf16[8,128,1024]{2,1,0:T(8,128)(2,1)S(1)} %copy-done, s32[1024]{0:T(1024)S(1)} %pad_clamp_fusion), kind=kCustom, calls=%fused_computation | custom fusion | bytes 4194816 | tf_op jit(solution)/shard_map/jit(_take)/gather | solution.py:41
  16.2 1.8 select_bitcast_fusion
  18.0 2.4 copy.16
  20.5 0.0 copy-start.2
  20.5 0.0 copy-start.5
  20.5 0.0 copy-start.6
  20.5 0.0 copy-start.1
  20.5 17.0 %all-to-all-start = ((bf16[8,128,1024]{2,0,1:T(8,128)(2,1)}), bf16[8,128,1024]{2,0,1:T(8,128)(2,1)}, u32[]{:S(2)}, u32[]{:S(2)}) async-start(bf16[8,128,1024]{2,0,1:T(8,128)(2,1)} %copy.16), calls=%async_computation | async-start | bytes 4194304 | tf_op jit(solution)/shard_map/all_to_all | solution.py:42
  37.5 0.0 all-reduce.3.cloned.1.call-start
  37.6 0.0 copy-done.2
  37.6 0.6 fusion.11
  39.5 0.0 copy-done.5
  39.5 0.1 and_select_fusion.1
  39.6 0.8 fusion.14
  40.5 0.0 copy-done.6
  40.5 0.2 fusion.9
  40.7 0.2 fusion.8
  40.9 0.0 copy-done.1
  40.9 1.9 broadcast_multiply_fusion
  42.9 46.4 %all-to-all-done = bf16[8,128,1024]{2,0,1:T(8,128)(2,1)} async-done(((bf16[8,128,1024]{2,0,1:T(8,128)(2,1)}), bf16[8,128,1024]{2,0,1:T(8,128)(2,1)}, u32[]{:S(2)}, u32[]{:S(2)}) %all-to-all-start) | async-done | bytes 2097184 | tf_op jit(solution)/shard_map/all_to_all | solution.py:42
  89.3 0.0 copy-start.4
  89.3 0.0 copy-start.3
  89.3 3.4 %fusion.3 = f32[512,256]{1,0:T(8,128)} fusion(bf16[8,64,2,1024]{3,0,2,1:T(8,128)(2,1)} %bitcast.1, bf16[256,2,1024]{2,1,0:T(2,128)(2,1)} %broadcast_multiply_fusion), kind=kOutput, calls=%fused_computation.5 | convolution fusion | flops 536870912 | bytes 3670016 | tf_op jit(solution)/shard_map/dot_general | solution.py:45
  92.7 0.0 all-reduce.3.cloned.1.call-update
  92.7 0.1 broadcast_add_fusion
  92.8 0.1 add.57
  92.9 1.3 dynamic-slice
  94.8 0.0 copy-done.4
  94.8 0.0 copy-done.3
  94.8 0.2 select_reduce_fusion
  95.1 153.1 %all-reduce.3.cloned.1.call-done = f32[512,256]{1,0:T(8,128)} async-done(((f32[512,256]{1,0:T(8,128)}), f32[512,256]{1,0:T(8,128)}) %all-reduce.3.cloned.1.call-update) | async-done | bytes 524304
  248.2 1.4 dynamic-slice_divide_fusion
  (5 shorter events, 0.0 us)
Async XLA Ops:
  6.5 1.6 copy-start
  20.5 17.1 %copy-start.2 = (s32[24]{0:T(128)S(1)}, s32[24]{0:T(128)}, u32[]{:S(2)}) copy-start(s32[24]{0:T(128)} %param.10) | copy-start | bytes 292
  20.5 19.0 %copy-start.5 = (s32[128]{0:T(128)S(1)}, s32[128]{0:T(128)}, u32[]{:S(2)}) copy-start(s32[128]{0:T(128)} %param.12) | copy-start | bytes 1540
  20.5 20.0 %copy-start.6 = (s32[128]{0:T(128)S(1)}, s32[128]{0:T(128)}, u32[]{:S(2)}) copy-start(s32[128]{0:T(128)} %param.11) | copy-start | bytes 1540
  20.5 20.4 %copy-start.1 = (bf16[256,2,1024]{2,1,0:T(2,128)(2,1)S(1)}, bf16[256,2,1024]{2,1,0:T(2,128)(2,1)}, u32[]{:S(2)}) copy-start(bf16[256,2,1024]{2,1,0:T(2,128)(2,1)} %param.9) | copy-start | bytes 3145732
  20.5 68.8 %all-to-all-start = ((bf16[8,128,1024]{2,0,1:T(8,128)(2,1)}), bf16[8,128,1024]{2,0,1:T(8,128)(2,1)}, u32[]{:S(2)}, u32[]{:S(2)}) async-start(bf16[8,128,1024]{2,0,1:T(8,128)(2,1)} %copy.16), calls=%async_computation | async-start | bytes 4194304 | tf_op jit(solution)/shard_map/all_to_all | solution.py:42
  37.5 210.7 %all-reduce.3.cloned.1.call-start = ((), (), s32[]{:S(2)}) async-start(), calls=%async_computation.1 | async-start | bytes 1048576
  89.3 5.5 %copy-start.4 = (s32[8,2]{0,1:T(2,128)S(1)}, s32[8,2]{0,1:T(2,128)}, u32[]{:S(2)}) copy-start(s32[8,2]{0,1:T(2,128)} %param.13) | copy-start | bytes 196
  89.3 5.6 %copy-start.3 = (f32[300]{0:T(512)S(1)}, f32[300]{0:T(512)}, u32[]{:S(2)}) copy-start(f32[300]{0:T(512)} %param.14) | copy-start | bytes 3604
Sparse Core Ops, SparseCore 0:
  92.9 155.2 all-reduce.2
where the time goes:
time: 257 us; the launch traced here: 256 us
  waiting for transfers between devices  200 us (78%)
  starting transfers between devices  17 us (7%)
  between operations  15.5 us (6%)
  local copies, waits for them, and re-layouts  12.8 us (5%)
  other arithmetic  8.06 us (3%)
  matrix products  3.44 us (1%)
    unnamed x2, waiting for transfers between devices  153 us
    all_to_all x1, waiting for transfers between devices, on_device(): lax.all_to_all(ordered, 'pair', split_axis=1, concat_axis=0, tiled=True)  46.4 us
    all_to_all x1, starting transfers between devices, on_device(): lax.all_to_all(ordered, 'pair', split_axis=1, concat_axis=0, tiled=True)  17 us
    gather x1, local copies, waits for them, and re-layouts, on_device(): ordered = jnp.take(amplitudes, slot_tiles, axis=1)  8.06 us
  transfers between devices with their start and end apart: 2, of which 2 were waited for; matrix products, arithmetic and copies ran while one was open for 2% of the time, Pallas kernels for 0%

commit v1 on v0

--- a/solution.py
+++ b/solution.py
@@ -39,7 +39,10 @@
         screening, my_slots
     ).astype(jnp.float32)
     ordered = jnp.take(amplitudes, slot_tiles, axis=1)
-    columns = lax.all_to_all(ordered, "pair", split_axis=1, concat_axis=0, tiled=True)
+    size = lax.axis_size("pair")
+    blocks = jnp.stack(jnp.split(ordered, size, axis=1), axis=0)
+    blocks = lax.all_to_all(blocks, "pair", split_axis=0, concat_axis=0)
+    columns = jnp.concatenate(blocks, axis=0)
     masked_ints = integrals * keep.astype(jnp.bfloat16)[None, :, None]
     ladder = lax.psum_scatter(
         lax.dot_general(

time: 257 us -> 295 us (1.15)
  local copies, waits for them, and re-layouts: 12.8 us -> 51 us
    unnamed x15 -> x78, local copies, waits for them, and re-layouts: 1.42 us -> 41.4 us
where the time goes in v1:
time: 295 us
  waiting for transfers between devices  200 us (68%)
  local copies, waits for them, and re-layouts  51 us (17%)
  starting transfers between devices  17 us (6%)
  between operations  15.5 us (5%)
  other arithmetic  8.06 us (3%)
  matrix products  3.41 us (1%)
    unnamed x2, waiting for transfers between devices  153 us
    all_to_all x1, waiting for transfers between devices, on_device(): blocks = lax.all_to_all(blocks, 'pair', split_axis=0, concat_axis=0)  46.4 us
    unnamed x78, local copies, waits for them, and re-layouts  41.4 us
    all_to_all x1, starting transfers between devices, on_device(): blocks = lax.all_to_all(blocks, 'pair', split_axis=0, concat_axis=0)  17 us
    gather x1, local copies, waits for them, and re-layouts, on_device(): ordered = jnp.take(amplitudes, slot_tiles, axis=1)  8.06 us
  transfers between devices with their start and end apart: 2, of which 2 were waited for; matrix products, arithmetic and copies ran while one was open for 2% of the time, Pallas kernels for 0%

profile of v1, /device:TPU:2, one launch (start us, length us, event | category | flops | bytes accessed | tf_op | source)
XLA Modules:
  0.0 294.5 jit_solution(4494192678080528583)
XLA Ops:
  6.5 0.8 compare_select_fusion
  7.3 0.7 compare_and_fusion
  8.1 8.1 %gather_fusion = bf16[128,8,1024]{2,0,1:T(8,128)(2,1)} fusion(bf16[8,128,1024]{2,1,0:T(8,128)(2,1)S(1)} %copy-done, s32[1024]{0:T(1024)S(1)} %pad_clamp_fusion), kind=kCustom, calls=%fused_computation | custom fusion | bytes 4194816 | tf_op jit(solution)/shard_map/jit(_take)/gather | solution.py:41
  16.2 1.8 select_bitcast_fusion
  18.7 0.6 constant_dynamic-update-slice_fusion.62
  21.2 0.6 constant_dynamic-update-slice_fusion.58
  21.8 0.6 constant_dynamic-update-slice_fusion.57
  22.5 0.6 constant_dynamic-update-slice_fusion.56
  23.7 0.6 constant_dynamic-update-slice_fusion.54
  24.4 0.6 constant_dynamic-update-slice_fusion.53
  25.0 0.6 constant_dynamic-update-slice_fusion.52
  26.3 0.6 constant_dynamic-update-slice_fusion.50
  26.9 0.6 constant_dynamic-update-slice_fusion.49
  27.6 0.6 constant_dynamic-update-slice_fusion.48
  28.8 0.6 constant_dynamic-update-slice_fusion.46
  30.1 0.6 constant_dynamic-update-slice_fusion.44
  31.4 0.6 constant_dynamic-update-slice_fusion.42
  32.0 0.7 constant_dynamic-update-slice_fusion.41
  32.7 0.6 constant_dynamic-update-slice_fusion.40
  33.9 0.6 constant_dynamic-update-slice_fusion.38
  34.6 0.6 constant_dynamic-update-slice_fusion.37
  36.4 0.6 constant_dynamic-update-slice_fusion.34
  39.0 0.6 constant_dynamic-update-slice_fusion.30
  39.6 0.6 constant_dynamic-update-slice_fusion.29
  40.3 0.6 constant_dynamic-update-slice_fusion.28
  41.5 0.6 constant_dynamic-update-slice_fusion.26
  42.2 0.6 constant_dynamic-update-slice_fusion.25
  42.8 0.6 constant_dynamic-update-slice_fusion.24
  44.1 0.6 constant_dynamic-update-slice_fusion.22
  45.3 0.6 constant_dynamic-update-slice_fusion.20
  46.6 0.6 constant_dynamic-update-slice_fusion.18
  47.9 0.6 constant_dynamic-update-slice_fusion.16
  49.1 0.6 constant_dynamic-update-slice_fusion.14
  49.8 0.6 constant_dynamic-update-slice_fusion.13
  51.7 0.7 constant_dynamic-update-slice_fusion.10
  52.3 0.6 constant_dynamic-update-slice_fusion.9
  53.0 0.6 constant_dynamic-update-slice_fusion.8
  55.5 0.6 constant_dynamic-update-slice_fusion.4
  56.8 0.6 constant_dynamic-update-slice_fusion.2
  58.7 17.0 %all-to-all-start = ((bf16[64,8,2,1024]{3,2,1,0:T(2,128)(2,1)}), bf16[64,8,2,1024]{3,2,1,0:T(2,128)(2,1)}, u32[]{:S(2)}, u32[]{:S(2)}) async-start(bf16[64,8,2,1024]{3,2,1,0:T(2,128)(2,1)} %constant_dynamic-update-slice_fusion), calls=%async_computation | async-start | bytes 4194304 | tf_op jit(solution)/shard_map/all_to_all | solution.py:44
  75.8 0.6 fusion.11
  77.8 0.8 fusion.14
  79.1 1.9 broadcast_multiply_fusion
  81.0 46.4 %all-to-all-done = bf16[64,8,2,1024]{3,2,1,0:T(2,128)(2,1)} async-done(((bf16[64,8,2,1024]{3,2,1,0:T(2,128)(2,1)}), bf16[64,8,2,1024]{3,2,1,0:T(2,128)(2,1)}, u32[]{:S(2)}, u32[]{:S(2)}) %all-to-all-start) | async-done | bytes 2097184 | tf_op jit(solution)/shard_map/all_to_all | solution.py:44
  127.5 3.4 %fusion.3 = f32[512,256]{1,0:T(8,128)} fusion(bf16[64,8,2,1024]{3,2,1,0:T(2,128)(2,1)} %all-to-all-done, bf16[256,2,1024]{2,1,0:T(2,128)(2,1)} %broadcast_multiply_fusion), kind=kOutput, calls=%fused_computation.5 | convolution fusion | flops 536870912 | bytes 3670016 | tf_op jit(solution)/shard_map/dot_general | solution.py:48
  131.3 1.3 dynamic-slice
  133.2 153.1 %all-reduce.3.cloned.1.call-done = f32[512,256]{1,0:T(8,128)} async-done(((f32[512,256]{1,0:T(8,128)}), f32[512,256]{1,0:T(8,128)}) %all-reduce.3.cloned.1.call-update) | async-done | bytes 524304
  286.3 1.4 dynamic-slice_divide_fusion
  (56 shorter events, 19.3 us)
Async XLA Ops:
  6.5 1.6 copy-start
  58.7 17.1 %copy-start.2 = (s32[24]{0:T(128)S(1)}, s32[24]{0:T(128)}, u32[]{:S(2)}) copy-start(s32[24]{0:T(128)} %param.10) | copy-start | bytes 292
  58.7 19.0 %copy-start.5 = (s32[128]{0:T(128)S(1)}, s32[128]{0:T(128)}, u32[]{:S(2)}) copy-start(s32[128]{0:T(128)} %param.12) | copy-start | bytes 1540
  58.7 20.0 %copy-start.6 = (s32[128]{0:T(128)S(1)}, s32[128]{0:T(128)}, u32[]{:S(2)}) copy-start(s32[128]{0:T(128)} %param.11) | copy-start | bytes 1540
  58.7 20.4 %copy-start.1 = (bf16[256,2,1024]{2,1,0:T(2,128)(2,1)S(1)}, bf16[256,2,1024]{2,1,0:T(2,128)(2,1)}, u32[]{:S(2)}) copy-start(bf16[256,2,1024]{2,1,0:T(2,128)(2,1)} %param.9) | copy-start | bytes 3145732
  58.7 68.8 %all-to-all-start = ((bf16[64,8,2,1024]{3,2,1,0:T(2,128)(2,1)}), bf16[64,8,2,1024]{3,2,1,0:T(2,128)(2,1)}, u32[]{:S(2)}, u32[]{:S(2)}) async-start(bf16[64,8,2,1024]{3,2,1,0:T(2,128)(2,1)} %constant_dynamic-update-slice_fusion), calls=%async_computation | async-start | bytes 4194304 | tf_op jit(solution)/shard_map/all_to_all | solution.py:44
  75.7 210.6 %all-reduce.3.cloned.1.call-start = ((), (), s32[]{:S(2)}) async-start(), calls=%async_computation.1 | async-start | bytes 1048576
  81.0 50.0 %copy-start.4 = (s32[8,2]{0,1:T(2,128)S(1)}, s32[8,2]{0,1:T(2,128)}, u32[]{:S(2)}) copy-start(s32[8,2]{0,1:T(2,128)} %param.13) | copy-start | bytes 196
  81.0 50.0 %copy-start.3 = (f32[300]{0:T(512)S(1)}, f32[300]{0:T(512)}, u32[]{:S(2)}) copy-start(f32[300]{0:T(512)} %param.14) | copy-start | bytes 3604
Sparse Core Ops, SparseCore 0:
  131.0 155.2 all-reduce.2
